TPU v7x, 128 devices: a whole 4x4x4 slice. The times are simulated.
128 devices in a mesh: row: 8 (over x, core), col: 16 (over z, y).
Axes of the slice: x: 4, y: 4, z: 4, core: 2. Of those that a mesh axis runs over, the one named last changes fastest.
Arguments:
- amplitudes: bfloat16 [16, 16, 512, 512], P(None, 'row', 'col'), may hold values from -6 to 6
- integrals: bfloat16 [16, 512, 16, 512], P('row', 'col'), may hold values from -0.09375 to 0.09375
- occupancy: int32 [16, 16, 4, 4], replicated, may hold values from 0 to 1, as said below
Outputs:
- cycle: bfloat16 [16, 16, 512, 512], P('col', 'row')
Inputs may be any that keep to these rules, and one draw needn't show every extreme that they name: occupancy[i, k, s, t] is 1 where tile s of the first virtual index and tile t of the second are kept for the pair (i, k), else 0; it is always 1 for i = k.
All inputs are finite; a program needn't handle non-finite values.
Results may differ from a plain program's by a relative error of at most 0.001.
Values may be sent and summed in bfloat16 or wider, within the bound.
No kernel may reach another device: no remote copies, remote signals or barrier semaphores. Data moves between devices by JAX's collectives and lax.ppermute only.
A program may use at most 128 MiB of HBM per device.

v0:
```python
import jax
import jax.numpy as jnp
from jax import lax
from jax.sharding import PartitionSpec as P

DOM = 4
TILE = 128


def screen(amplitudes, occupancy):
    k_rows = amplitudes.shape[1]
    c_rows = amplitudes.shape[2]
    k_first = lax.axis_index("row") * k_rows
    c_first = lax.axis_index("col") * c_rows
    occ_rows = lax.dynamic_slice_in_dim(occupancy, k_first, k_rows, 1).astype(jnp.float32)
    c_tiles = (c_first + jnp.arange(c_rows, dtype=jnp.int32)) // TILE
    picker = (c_tiles[:, None] == jnp.arange(DOM, dtype=jnp.int32)[None, :]).astype(jnp.float32)
    tile_rows = jnp.einsum("cs,ikst->ikct", picker, occ_rows)
    mask_full = jnp.repeat(tile_rows, TILE, axis=3).astype(jnp.bfloat16)
    return amplitudes * mask_full


def per_device(amplitudes, integrals, occupancy):
    screened = screen(amplitudes, occupancy)
    regrouped = lax.all_to_all(screened, "row", split_axis=0, concat_axis=1, tiled=True)
    turned = lax.all_to_all(integrals, "col", split_axis=2, concat_axis=1, tiled=True)
    complete = lax.all_gather(turned, "row", axis=0, tiled=True)
    summed = jnp.einsum(
        "ikca,kcjb->jiba",
        lax.all_gather(regrouped, "col", axis=2, tiled=True),
        complete,
        preferred_element_type=jnp.float32,
    )
    return summed.astype(jnp.bfloat16)


def solution(mesh):
    in_specs = (P(None, "row", "col", None), P("row", "col", None, None), P())
    out_specs = P("col", "row", None, None)
    return jax.shard_map(
        per_device, mesh=mesh, in_specs=in_specs, out_specs=out_specs, check_vma=False
    )
```

profile of v0, /device:TPU:1, one launch (start us, length us, event | category | flops | bytes accessed | tf_op | source)
XLA Modules:
  0.0 225.8 jit_solution(14420888662035065762)
XLA Ops:
  6.5 0.0 copy-start
  6.5 0.0 copy-start.1
  6.5 0.0 all-gather.5.cloned.1.call-start
  6.5 1.9 copy.17
  8.4 24.4 %all_to_all.36 = bf16[2,32,16,512]{3,1,0,2:T(8,128)(2,1)S(1)} all-to-all(bf16[2,32,16,512]{3,1,0,2:T(8,128)(2,1)S(1)} %copy.17), channel_id=1, replica_groups=mesh['row'=8,'col'=16] {'col'}, dimensions={2} | all-to-all | bytes 2097152 | tf_op jit(solution)/shard_map/all_to_all | solution.py:26
  32.9 1.1 copy.18
  34.0 0.0 all-gather.5.cloned.1.call-update
  34.0 0.0 all-gather.3.cloned.1.call-start
  34.1 0.0 copy-done
  34.1 0.1 constant_dynamic-slice_fusion
  34.2 0.2 copy.23
  34.4 0.2 fusion.7
  34.6 0.3 copy.15
  34.9 1.3 broadcast_in_dim.2
  36.2 0.4 convert_element_type.29
  36.6 0.0 copy-done.1
  36.6 0.4 mul.11
  37.0 32.1 %all_to_all.37 = bf16[16,2,32,512]{3,2,1,0:T(8,128)(2,1)S(1)} all-to-all(bf16[16,2,32,512]{3,2,1,0:T(8,128)(2,1)S(1)} %mul.11), channel_id=1, replica_groups=mesh['row'=8,'col'=16] {'row'}, dimensions={0} | all-to-all | bytes 2097152 | tf_op jit(solution)/shard_map/all_to_all | solution.py:25
  69.1 1.1 copy.16
  70.1 0.0 all-gather.3.cloned.1.call-update
  70.2 23.9 %all-gather.5.cloned.1.call-done = bf16[16,512,1,512]{3,1,2,0:T(8,128)(2,1)} async-done(((bf16[2,512,1,512]{3,1,2,0:T(8,128)(2,1)}), bf16[16,512,1,512]{3,1,2,0:T(8,128)(2,1)}) %all-gather.5.cloned.1.call-update) | async-done | bytes 8388624 | tf_op jit(solution)/shard_map/all_gather | solution.py:27
  94.1 108.7 %all-gather.3.cloned.1.call-done = bf16[2,16,512,512]{3,2,1,0:T(8,128)(2,1)} async-done(((bf16[2,16,32,512]{3,2,1,0:T(8,128)(2,1)}), bf16[2,16,512,512]{3,2,1,0:T(8,128)(2,1)}) %all-gather.3.cloned.1.call-update) | async-done | bytes 16777232 | tf_op jit(solution)/shard_map/all_gather | solution.py:30
  202.8 14.8 %fusion.4 = bf16[1,2,512,512]{2,3,1,0:T(8,128)(2,1)S(1)} fusion(bf16[2,16,512,512]{3,2,1,0:T(8,128)(2,1)} %all-gather.3.cloned.1.call-done, bf16[16,512,1,512]{3,1,2,0:T(8,128)(2,1)} %all-gather.5.cloned.1.call-done), kind=kOutput, calls=%fused_computation.3 | convolution fusion | flops 8590458880 | bytes 26214400 | tf_op jit(solution)/shard_map/ikca,kcjb->jiba/dot_general | solution.py:28
  217.6 1.3 copy.20
  (1 shorter events, 0.0 us)
Async XLA Ops:
  6.5 27.5 %copy-start = (s32[16,16,4,4]{1,3,2,0:T(4,128)S(1)}, s32[16,16,4,4]{1,3,2,0:T(4,128)}, u32[]{:S(2)}) copy-start(s32[16,16,4,4]{1,3,2,0:T(4,128)} %param.5) | copy-start | bytes 49156
  6.5 30.1 %copy-start.1 = (bf16[16,2,32,512]{3,2,1,0:T(8,128)(2,1)S(1)}, bf16[16,2,32,512]{3,2,1,0:T(8,128)(2,1)}, u32[]{:S(2)}) copy-start(bf16[16,2,32,512]{3,2,1,0:T(8,128)(2,1)} %param.3) | copy-start | bytes 3145732
  6.5 87.5 %all-gather.5.cloned.1.call-start = ((), (), s32[]{:S(2)}) async-start(), calls=%async_computation.3 | async-start | bytes 9437184 | tf_op jit(solution)/shard_map/all_gather | solution.py:27
  34.0 168.8 %all-gather.3.cloned.1.call-start = ((), (), s32[]{:S(2)}) async-start(), calls=%async_computation.2 | async-start | bytes 17825792 | tf_op jit(solution)/shard_map/all_gather | solution.py:30
Sparse Core Ops, SparseCore 0:
  34.1 59.8 all-gather.4
  96.2 106.5 all-gather.2
where the time goes:
time: 226 us
  waiting for transfers between devices  133 us (59%)
  blocking collectives  56.5 us (25%)
  matrix products  15 us (7%)
  between operations  13.5 us (6%)
  local copies, waits for them, and re-layouts  7.75 us (3%)
    all_gather x1, waiting for transfers between devices, per_device(): lax.all_gather(regrouped, 'col', axis=2, tiled=True)  109 us
    all_to_all x1, blocking collectives, per_device(): lax.all_to_all(screened, 'row', split_axis=0, concat_axis=1, tiled=True)  32.1 us
    all_to_all x1, blocking collectives, per_device(): lax.all_to_all(integrals, 'col', split_axis=2, concat_axis=1, tiled=True)  24.4 us
    all_gather x1, waiting for transfers between devices, per_device(): complete = lax.all_gather(turned, 'row', axis=0, tiled=True)  23.9 us
    dot_general x1, matrix products, per_device(): jnp.einsum('ikca,kcjb->jiba', lax.all_gather(regrouped, 'col', axis=2, ti...  14.8 us
  transfers between devices with their start and end apart: 2, of which 2 were waited for; matrix products, arithmetic and copies ran while one was open for 2% of the time, Pallas kernels for 0%

commit v1 on v0

v1 whole, which is shorter than its diff:
```python
import jax
import jax.numpy as jnp
from jax import lax
from jax.experimental import pallas as pl
from jax.experimental.pallas import tpu as pltpu
from jax.sharding import PartitionSpec as P


TILE = 128
SHIFTS = (0, 1, 3, 2)


def x_move(value, shift):
    pairs = [(2 * x + h, 2 * ((x + shift) % 4) + h) for x in range(4) for h in range(2)]
    return lax.ppermute(value, "row", pairs)


def core_swap(value):
    return lax.ppermute(value, "row", [(r, r ^ 1) for r in range(8)])


def y_move(value, shift):
    pairs = [(4 * z + y, 4 * z + (y + shift) % 4) for z in range(4) for y in range(4)]
    return lax.ppermute(value, "col", pairs)


def z_move(value, shift):
    pairs = [(4 * z + y, 4 * ((z + shift) % 4) + y) for z in range(4) for y in range(4)]
    return lax.ppermute(value, "col", pairs)


def screen_body(occ_ref, amp_ref, *out_refs):
    row, col = lax.axis_index("row"), lax.axis_index("col")
    x, h, z = row // 2, row % 2, col // 4
    table = occ_ref[:, pl.ds(z, 1), :, :].reshape(16, 4, 16)
    orbital = lax.broadcasted_iota(jnp.int32, (16, 4, 16), 2)
    for k in range(2):
        kept = jnp.sum(jnp.where(orbital == 2 * row + k, table, 0), axis=2, keepdims=True)
        mask_ref = out_refs[4]
        mask_ref[k] = jnp.broadcast_to(kept.astype(jnp.float32), (16, 4, TILE))
    for d, shift in enumerate(SHIFTS):
        for e in range(2):
            first = 4 * ((x + shift) % 4) + 2 * (h if e == 0 else 1 - h)
            for i in range(2):
                for k in range(2):
                    rows = out_refs[4][k, first + i]
                    for t in range(4):
                        part = amp_ref[first + i, k, :, TILE * t : TILE * (t + 1)]
                        keep = jnp.broadcast_to(rows[t : t + 1], (32, TILE)).astype(jnp.bfloat16)
                        out_refs[d][e, i, k, :, TILE * t : TILE * (t + 1)] = part * keep


def screen(occupancy, amplitudes):
    piece = jax.ShapeDtypeStruct((2, 2, 2, 32, 512), jnp.bfloat16)
    vmem = pl.BlockSpec(memory_space=pltpu.VMEM)
    return pl.pallas_call(
        screen_body,
        out_shape=[piece] * 4,
        in_specs=[vmem, vmem],
        out_specs=[vmem] * 4,
        scratch_shapes=[pltpu.VMEM((2, 16, 4, TILE), jnp.float32)],
        cost_estimate=pl.CostEstimate(flops=1 << 19, bytes_accessed=1 << 21, transcendentals=0),
    )(jnp.transpose(occupancy, (0, 2, 3, 1)), amplitudes)


def ring(value, move):
    forth = move(value, 1)
    back = move(value, -1)
    far_forth = move(forth[:, 0], 1)
    far_back = move(back[:, 1], -1)
    return [[value[:, i], forth[:, i], back[:, i], (far_forth, far_back)[i]] for i in range(2)]


def split_ring(values, move):
    near = [[None, None], [None, None]]
    for way, order in (("forth", (0, 1)), ("back", (1, 0))):
        for i in order:
            near[i][0 if way == "forth" else 1] = move(values[i], 1 if way == "forth" else -1)
    far = [move(near[0][0], 1), move(near[1][1], -1)]
    return [[values[i], near[i][0], near[i][1], far[i]] for i in range(2)]


def per_device(amplitudes, integrals, occupancy):
    col = lax.axis_index("col")
    z, y = col // 4, col % 4

    ready = screen(occupancy, amplitudes)
    arrived = [x_move(ready[d], shift) if shift else ready[d] for d, shift in enumerate(SHIFTS)]

    by_orbital = jnp.transpose(integrals, (2, 0, 1, 3)).reshape(4, 4, 2, 32, 512)
    over_z = []
    for shift in SHIFTS:
        piece = lax.dynamic_index_in_dim(by_orbital, (z + shift) % 4, 0, keepdims=False)
        over_z.append(z_move(piece, shift) if shift else piece)
    over_y = []
    for shift in SHIFTS:
        piece = jnp.stack([lax.dynamic_index_in_dim(p, (y + shift) % 4, 0, keepdims=False) for p in over_z])
        over_y.append(y_move(piece, shift) if shift else piece)
    held = jnp.stack(over_y)
    forth, back = x_move(held, 1), x_move(held, -1)
    far = jnp.concatenate([x_move(forth[:2], 1), x_move(back[2:], -1)], axis=0)
    mine = [held, forth, back, far]
    other = []
    for piece in mine:
        other.append(core_swap(piece))
    b_mine = jnp.stack(mine).transpose(2, 1, 0, 3, 4, 5).reshape(4, 1024, 512)
    b_other = jnp.stack(other).transpose(1, 2, 0, 3, 4, 5).reshape(4, 1024, 512)

    half_own = jnp.stack([p[0] for p in arrived])
    half_other = core_swap(jnp.stack([p[1] for p in arrived]))
    own = [jnp.stack(p) for p in ring(half_own, y_move)]
    oth = [jnp.stack(p) for p in ring(half_other, z_move)]
    own_pieces = split_ring(own, z_move)
    oth_pieces = split_ring(oth, y_move)

    outs = []
    for i in range(2):
        total = None
        for step in (0, 1 + i, 2 - i, 3):
            for pieces, right in ((own_pieces, b_mine), (oth_pieces, b_other)):
                left = pieces[i][step].reshape(1024, 512)
                product = lax.dot_general(
                    right[step], left, (((0,), (0,)), ((), ())), preferred_element_type=jnp.float32
                )
                total = product if total is None else total + product
        outs.append(total.astype(jnp.bfloat16))
    return jnp.stack(outs)[None]


def solution(mesh):
    in_specs = (P(None, "row", "col", None), P("row", "col", None, None), P())
    out_specs = P("col", "row", None, None)
    return jax.shard_map(per_device, mesh=mesh, in_specs=in_specs, out_specs=out_specs, check_vma=False)
```

time: 226 us -> 190 us (0.84)
  blocking collectives: 56.5 us -> 0 us
  starting transfers between devices: 0.04 us -> 46.8 us
  waiting for transfers between devices: 133 us -> 118 us
  between operations: 13.5 us -> 0.72 us
  matrix products: 15 us -> 12 us
  other arithmetic: 0.37 us -> 3.16 us
  Pallas kernels: 0 us -> 2.49 us
    all_gather x2 -> x0, waiting for transfers between devices: 133 us -> none  [the longest x1 109 us: per_device(): lax.all_gather(regrouped, 'col', axis=2, tiled=True)]
    ppermute x0 -> x38, waiting for transfers between devices: none -> 118 us  [the longest x13 58.9 us: y_move(): return lax.ppermute(value, 'col', pairs)]
    all_to_all x2 -> x0, blocking collectives: 56.5 us -> none  [the longest x1 32.1 us: per_device(): lax.all_to_all(screened, 'row', split_axis=0, concat_axis=1, tiled=True)]
    ppermute x0 -> x38, starting transfers between devices: none -> 46.8 us  [the longest x13 14.4 us: y_move(): return lax.ppermute(value, 'col', pairs)]
    slice x0 -> x16, local copies, waits for them, and re-layouts: none -> 3.08 us  [the longest x10 1.96 us: per_device(): right[step]]
    dot_general x2 -> x16, matrix products: 15 us -> 12 us  [per_device(): lax.dot_general(right[step], left, (((0,), (0,)), ((), ())), preferred_el...]
    pallas_call x0 -> x1, Pallas kernels: none -> 2.49 us  [screen(): pl.pallas_call(screen_body, out_shape=[piece] * 4, in_specs=[vmem, vmem],...]
  transfers between devices with their start and end apart: 2 -> 38, of which waited for: 2 -> 12; matrix products, arithmetic and copies ran while one was open for 2% -> 9% of each run, Pallas kernels for 0% -> 1%
where the time goes in v1:
time: 190 us; the launch traced here: 188 us
  waiting for transfers between devices  118 us (62%)
  starting transfers between devices  46.8 us (25%)
  matrix products  12 us (6%)
  local copies, waits for them, and re-layouts  5.59 us (3%)
  other arithmetic  3.16 us (2%)
  Pallas kernels  2.49 us (1%)
    ppermute x13, waiting for transfers between devices, y_move(): return lax.ppermute(value, 'col', pairs)  58.9 us
    ppermute x13, waiting for transfers between devices, z_move(): return lax.ppermute(value, 'col', pairs)  57.9 us
    ppermute x13, starting transfers between devices, y_move(): return lax.ppermute(value, 'col', pairs)  14.4 us
    ppermute x13, starting transfers between devices, z_move(): return lax.ppermute(value, 'col', pairs)  13.4 us
    dot_general x16, matrix products, per_device(): lax.dot_general(right[step], left, (((0,), (0,)), ((), ())), preferred_el...  12 us
    ppermute x7, starting transfers between devices, x_move(): return lax.ppermute(value, 'row', pairs)  9.61 us
    ppermute x5, starting transfers between devices, core_swap(): return lax.ppermute(value, 'row', [(r, r ^ 1) for r in range(8)])  9.47 us
  transfers between devices with their start and end apart: 38, of which 12 were waited for; matrix products, arithmetic and copies ran while one was open for 9% of the time, Pallas kernels for 1%

profile of v1, /device:TPU:1, one launch (start us, length us, event | category | flops | bytes accessed | tf_op | source)
XLA Modules:
  0.0 188.4 jit_solution(749557816785488533)
XLA Ops:
  0.0 1.8 copy.10
  1.9 2.5 %collective-permute-start = (bf16[4,2,32,512]{3,2,1,0:T(8,128)(2,1)S(1)}, bf16[4,2,32,512]{3,2,1,0:T(8,128)(2,1)S(1)}, u32[]{:S(2)}, u32[]{:S(2)}) collective-permute-start(bf16[4,2,32,512]{3,2,1,0:T(8,128)(2,1)S(1)} %get-tuple-element.27), channel_id=1, source_target_pairs={{0,4},{1,5},{2,6},{3,7},{4,8},{5,9},{6,10},{7,11},{8,12},{9,13},{1... | collective-permute-start | bytes 786440 | tf_op jit(solution)/shard_map/ppermute | solution.py:29
  4.4 2.2 %collective-permute-start.1 = (bf16[4,2,32,512]{3,2,1,0:T(8,128)(2,1)S(1)}, bf16[4,2,32,512]{3,2,1,0:T(8,128)(2,1)S(1)}, u32[]{:S(2)}, u32[]{:S(2)}) collective-permute-start(bf16[4,2,32,512]{3,2,1,0:T(8,128)(2,1)S(1)} %get-tuple-element.29), channel_id=1, source_target_pairs={{0,12},{1,13},{2,14},{3,15},{4,0},{5,1},{6,2},{7,3},{8,4},{9,5},{1... | collective-permute-start | bytes 786440 | tf_op jit(solution)/shard_map/ppermute | solution.py:29
  7.9 2.5 %shard_map.37 = (bf16[2,2,2,32,512]{4,3,2,1,0:T(8,128)(2,1)}, bf16[2,2,2,32,512]{4,3,2,1,0:T(8,128)(2,1)}, bf16[2,2,2,32,512]{4,3,2,1,0:T(8,128)(2,1)}, bf16[2,2,2,32,512]{4,3,2,1,0:T(8,128)(2,1)}) custom-call(s32[16,4,4,16]{3,2,1,0:T(4,128)} %bitcast.174, bf16[16,2,32,512]{3,2,1,0:T(8,128)(2,1)} %amp_ref.1), custom_call_target="tpu_custom_call" | custom-call | flops 524288 | bytes 2097152 | tf_op jit(solution)/shard_map/pallas_call | solution.py:56
  14.2 1.6 collective-permute-start.12
  15.9 3.2 %collective-permute-done.2 = bf16[4,2,32,512]{3,2,1,0:T(8,128)(2,1)S(1)} collective-permute-done((bf16[4,2,32,512]{3,2,1,0:T(8,128)(2,1)S(1)}, bf16[4,2,32,512]{3,2,1,0:T(8,128)(2,1)S(1)}, u32[]{:S(2)}, u32[]{:S(2)}) %collective-permute-start.2) | collective-permute-done | bytes 262176 | tf_op jit(solution)/shard_map/ppermute | solution.py:29
  22.1 1.7 collective-permute-start.5
  24.8 2.4 %collective-permute-start.20 = (bf16[4,2,2,32,512]{4,3,2,1,0:T(8,128)(2,1)S(1)}, bf16[4,2,2,32,512]{4,3,2,1,0:T(8,128)(2,1)S(1)}, u32[]{:S(2)}, u32[]{:S(2)}) collective-permute-start(bf16[4,2,2,32,512]{4,3,2,1,0:T(8,128)(2,1)S(1)} %pad_maximum_fusion.6), channel_id=1, source_target_pairs={{0,16},{16,0},{32,48},{48,32},{64,80},{80,64},{96,112},{112,96},{1... | collective-permute-start | bytes 1572872 | tf_op jit(solution)/shard_map/ppermute | solution.py:19
  30.4 3.3 %collective-permute-done.5 = bf16[4,2,32,512]{3,2,1,0:T(8,128)(2,1)S(1)} collective-permute-done((bf16[4,2,32,512]{3,2,1,0:T(8,128)(2,1)S(1)}, bf16[4,2,32,512]{3,2,1,0:T(8,128)(2,1)S(1)}, u32[]{:S(2)}, u32[]{:S(2)}) %collective-permute-start.5) | collective-permute-done | bytes 262176 | tf_op jit(solution)/shard_map/ppermute | solution.py:24
  37.0 9.4 %collective-permute-done.13 = bf16[4,2,2,32,512]{4,3,2,0,1:T(8,128)(2,1)S(1)} collective-permute-done((bf16[4,2,2,32,512]{4,3,2,0,1:T(8,128)(2,1)S(1)}, bf16[4,2,2,32,512]{4,3,2,0,1:T(8,128)(2,1)S(1)}, u32[]{:S(2)}, u32[]{:S(2)}) %collective-permute-start.13) | collective-permute-done | bytes 524320 | tf_op jit(solution)/shard_map/ppermute | solution.py:24
  46.9 8.0 %collective-permute-done.15 = bf16[4,2,32,512]{3,2,1,0:T(8,128)(2,1)S(1)} collective-permute-done((bf16[4,2,32,512]{3,2,1,0:T(8,128)(2,1)S(1)}, bf16[4,2,32,512]{3,2,1,0:T(8,128)(2,1)S(1)}, u32[]{:S(2)}, u32[]{:S(2)}) %collective-permute-start.15) | collective-permute-done | bytes 262176 | tf_op jit(solution)/shard_map/ppermute | solution.py:24
  56.8 2.5 %collective-permute-done.22 = bf16[4,2,2,32,512]{4,3,2,0,1:T(8,128)(2,1)S(1)} collective-permute-done((bf16[4,2,2,32,512]{4,3,2,0,1:T(8,128)(2,1)S(1)}, bf16[4,2,2,32,512]{4,3,2,0,1:T(8,128)(2,1)S(1)}, u32[]{:S(2)}, u32[]{:S(2)}) %collective-permute-start.22) | collective-permute-done | bytes 524320 | tf_op jit(solution)/shard_map/ppermute | solution.py:29
  60.4 1.6 collective-permute-start.31
  63.7 4.5 %collective-permute-start.16 = (bf16[4,4,2,32,512]{4,3,2,1,0:T(8,128)(2,1)S(1)}, bf16[4,4,2,32,512]{4,3,2,1,0:T(8,128)(2,1)S(1)}, u32[]{:S(2)}, u32[]{:S(2)}) collective-permute-start(bf16[4,4,2,32,512]{4,3,2,1,0:T(8,128)(2,1)S(1)} %get-tuple-element.22), channel_id=1, source_target_pairs={{0,16},{16,0},{32,48},{48,32},{64,80},{80,64},{96,112},{112,96},{1... | collective-permute-start | bytes 3145736 | tf_op jit(solution)/shard_map/ppermute | solution.py:19
  68.4 18.9 %collective-permute-done.31 = bf16[4,2,32,512]{3,2,1,0:T(8,128)(2,1)S(1)} collective-permute-done((bf16[4,2,32,512]{3,2,1,0:T(8,128)(2,1)S(1)}, bf16[4,2,32,512]{3,2,1,0:T(8,128)(2,1)S(1)}, u32[]{:S(2)}, u32[]{:S(2)}) %collective-permute-start.31) | collective-permute-done | bytes 262176 | tf_op jit(solution)/shard_map/ppermute | solution.py:29
  88.0 1.8 collective-permute-start.17
  92.9 18.9 %collective-permute-done.34 = bf16[4,4,2,32,512]{4,3,2,1,0:T(8,128)(2,1)S(1)} collective-permute-done((bf16[4,4,2,32,512]{4,3,2,1,0:T(8,128)(2,1)S(1)}, bf16[4,4,2,32,512]{4,3,2,1,0:T(8,128)(2,1)S(1)}, u32[]{:S(2)}, u32[]{:S(2)}) %collective-permute-start.34) | collective-permute-done | bytes 1048608 | tf_op jit(solution)/shard_map/ppermute | solution.py:29
  112.5 2.7 %collective-permute-start.32 = (bf16[4,4,2,32,512]{4,3,2,1,0:T(8,128)(2,1)S(1)}, bf16[4,4,2,32,512]{4,3,2,1,0:T(8,128)(2,1)S(1)}, u32[]{:S(2)}, u32[]{:S(2)}) collective-permute-start(bf16[4,4,2,32,512]{4,3,2,1,0:T(8,128)(2,1)S(1)} %pad_maximum_fusion.3), channel_id=1, source_target_pairs={{0,12},{1,13},{2,14},{3,15},{4,0},{5,1},{6,2},{7,3},{8,4},{9,5},{1... | collective-permute-start | bytes 3145736 | tf_op jit(solution)/shard_map/ppermute | solution.py:29
  115.3 2.7 %collective-permute-start.27 = (bf16[4,4,2,32,512]{4,3,2,1,0:T(8,128)(2,1)S(1)}, bf16[4,4,2,32,512]{4,3,2,1,0:T(8,128)(2,1)S(1)}, u32[]{:S(2)}, u32[]{:S(2)}) collective-permute-start(bf16[4,4,2,32,512]{4,3,2,1,0:T(8,128)(2,1)S(1)} %pad_maximum_fusion.2), channel_id=1, source_target_pairs={{0,3},{1,0},{2,1},{3,2},{4,7},{5,4},{6,5},{7,6},{8,11},{9,8},{10,9... | collective-permute-start | bytes 3145736 | tf_op jit(solution)/shard_map/ppermute | solution.py:24
  121.0 14.4 %collective-permute-done.24 = bf16[4,4,2,32,512]{4,3,2,1,0:T(8,128)(2,1)S(1)} collective-permute-done((bf16[4,4,2,32,512]{4,3,2,1,0:T(8,128)(2,1)S(1)}, bf16[4,4,2,32,512]{4,3,2,1,0:T(8,128)(2,1)S(1)}, u32[]{:S(2)}, u32[]{:S(2)}) %collective-permute-start.24) | collective-permute-done | bytes 1048608 | tf_op jit(solution)/shard_map/ppermute | solution.py:29
  135.4 2.9 %collective-permute-done.25 = bf16[4,4,2,32,512]{4,3,2,1,0:T(8,128)(2,1)S(1)} collective-permute-done((bf16[4,4,2,32,512]{4,3,2,1,0:T(8,128)(2,1)S(1)}, bf16[4,4,2,32,512]{4,3,2,1,0:T(8,128)(2,1)S(1)}, u32[]{:S(2)}, u32[]{:S(2)}) %collective-permute-start.25) | collective-permute-done | bytes 1048608 | tf_op jit(solution)/shard_map/ppermute | solution.py:24
  140.8 19.0 %collective-permute-done.33 = bf16[4,4,2,32,512]{4,3,2,1,0:T(8,128)(2,1)S(1)} collective-permute-done((bf16[4,4,2,32,512]{4,3,2,1,0:T(8,128)(2,1)S(1)}, bf16[4,4,2,32,512]{4,3,2,1,0:T(8,128)(2,1)S(1)}, u32[]{:S(2)}, u32[]{:S(2)}) %collective-permute-start.33) | collective-permute-done | bytes 1048608 | tf_op jit(solution)/shard_map/ppermute | solution.py:24
  159.8 3.4 %collective-permute-start.37 = (bf16[4,4,2,32,512]{4,3,2,1,0:T(8,128)(2,1)S(1)}, bf16[4,4,2,32,512]{4,3,2,1,0:T(8,128)(2,1)S(1)}, u32[]{:S(2)}, u32[]{:S(2)}) collective-permute-start(bf16[4,4,2,32,512]{4,3,2,1,0:T(8,128)(2,1)S(1)} %collective-permute-done.33), channel_id=1, source_target_pairs={{0,3},{1,0},{2,1},{3,2},{4,7},{5,4},{6,5},{7,6},{8,11},{9,8},{10,9... | collective-permute-start | bytes 3145736 | tf_op jit(solution)/shard_map/ppermute | solution.py:24
  167.9 16.4 %collective-permute-done.29 = bf16[4,4,2,32,512]{4,3,2,1,0:T(8,128)(2,1)S(1)} collective-permute-done((bf16[4,4,2,32,512]{4,3,2,1,0:T(8,128)(2,1)S(1)}, bf16[4,4,2,32,512]{4,3,2,1,0:T(8,128)(2,1)S(1)}, u32[]{:S(2)}, u32[]{:S(2)}) %collective-permute-start.29) | collective-permute-done | bytes 1048608 | tf_op jit(solution)/shard_map/ppermute | solution.py:24
  (117 shorter events, 39.3 us)
Async XLA Ops:
  27.4 19.0 %collective-permute-start.13 = (bf16[4,2,2,32,512]{4,3,2,0,1:T(8,128)(2,1)S(1)}, bf16[4,2,2,32,512]{4,3,2,0,1:T(8,128)(2,1)S(1)}, u32[]{:S(2)}, u32[]{:S(2)}) collective-permute-start(bf16[4,2,2,32,512]{4,3,2,0,1:T(8,128)(2,1)S(1)} %copy.12), channel_id=1, source_target_pairs={{0,1},{1,2},{2,3},{3,0},{4,5},{5,6},{6,7},{7,4},{8,9},{9,10},{10,1... | collective-permute-start | bytes 1572872 | tf_op jit(solution)/shard_map/ppermute | solution.py:24
  28.8 17.9 %collective-permute-start.14 = (bf16[4,2,2,32,512]{4,3,2,0,1:T(8,128)(2,1)S(1)}, bf16[4,2,2,32,512]{4,3,2,0,1:T(8,128)(2,1)S(1)}, u32[]{:S(2)}, u32[]{:S(2)}) collective-permute-start(bf16[4,2,2,32,512]{4,3,2,0,1:T(8,128)(2,1)S(1)} %copy.12), channel_id=1, source_target_pairs={{0,3},{1,0},{2,1},{3,2},{4,7},{5,4},{6,5},{7,6},{8,11},{9,8},{10,9... | collective-permute-start | bytes 1572872 | tf_op jit(solution)/shard_map/ppermute | solution.py:24
  33.8 21.8 %collective-permute-start.6 = (bf16[4,4,2,32,512]{4,3,2,1,0:T(8,128)(2,1)S(1)}, bf16[4,4,2,32,512]{4,3,2,1,0:T(8,128)(2,1)S(1)}, u32[]{:S(2)}, u32[]{:S(2)}) collective-permute-start(bf16[4,4,2,32,512]{4,3,2,1,0:T(8,128)(2,1)S(1)} %get-tuple-element.22), channel_id=1, source_target_pairs={{0,32},{16,48},{32,64},{48,80},{64,96},{80,112},{96,0},{112,16},{1... | collective-permute-start | bytes 3145736 | tf_op jit(solution)/shard_map/ppermute | solution.py:15
  35.1 25.3 %collective-permute-start.7 = (bf16[4,4,2,32,512]{4,3,2,1,0:T(8,128)(2,1)S(1)}, bf16[4,4,2,32,512]{4,3,2,1,0:T(8,128)(2,1)S(1)}, u32[]{:S(2)}, u32[]{:S(2)}) collective-permute-start(bf16[4,4,2,32,512]{4,3,2,1,0:T(8,128)(2,1)S(1)} %get-tuple-element.22), channel_id=1, source_target_pairs={{0,96},{16,112},{32,0},{48,16},{64,32},{80,48},{96,64},{112,80},{1... | collective-permute-start | bytes 3145736 | tf_op jit(solution)/shard_map/ppermute | solution.py:15
  36.6 18.4 %collective-permute-start.21 = (bf16[4,2,2,32,512]{4,3,2,0,1:T(8,128)(2,1)S(1)}, bf16[4,2,2,32,512]{4,3,2,0,1:T(8,128)(2,1)S(1)}, u32[]{:S(2)}, u32[]{:S(2)}) collective-permute-start(bf16[4,2,2,32,512]{4,3,2,0,1:T(8,128)(2,1)S(1)} %copy.16), channel_id=1, source_target_pairs={{0,4},{1,5},{2,6},{3,7},{4,8},{5,9},{6,10},{7,11},{8,12},{9,13},{1... | collective-permute-start | bytes 1572872 | tf_op jit(solution)/shard_map/ppermute | solution.py:29
  55.0 35.0 %collective-permute-start.26 = (bf16[4,4,2,32,512]{4,3,2,1,0:T(8,128)(2,1)S(1)}, bf16[4,4,2,32,512]{4,3,2,1,0:T(8,128)(2,1)S(1)}, u32[]{:S(2)}, u32[]{:S(2)}) collective-permute-start(bf16[4,4,2,32,512]{4,3,2,1,0:T(8,128)(2,1)S(1)} %pad_maximum_fusion.1), channel_id=1, source_target_pairs={{0,12},{1,13},{2,14},{3,15},{4,0},{5,1},{6,2},{7,3},{8,4},{9,5},{1... | collective-permute-start | bytes 3145736 | tf_op jit(solution)/shard_map/ppermute | solution.py:29
  59.2 28.7 %collective-permute-start.8 = (bf16[2,4,2,32,512]{4,3,2,1,0:T(8,128)(2,1)S(1)}, bf16[2,4,2,32,512]{4,3,2,1,0:T(8,128)(2,1)S(1)}, u32[]{:S(2)}, u32[]{:S(2)}) collective-permute-start(bf16[2,4,2,32,512]{4,3,2,1,0:T(8,128)(2,1)S(1)} %slice.140), channel_id=1, source_target_pairs={{0,32},{16,48},{32,64},{48,80},{64,96},{80,112},{96,0},{112,16},{1... | collective-permute-start | bytes 1572872 | tf_op jit(solution)/shard_map/ppermute | solution.py:15
  60.4 27.0 %collective-permute-start.31 = (bf16[4,2,32,512]{3,2,1,0:T(8,128)(2,1)S(1)}, bf16[4,2,32,512]{3,2,1,0:T(8,128)(2,1)S(1)}, u32[]{:S(2)}, u32[]{:S(2)}) collective-permute-start(bf16[4,2,32,512]{3,2,1,0:T(8,128)(2,1)S(1)} %get-tuple-element.40), channel_id=1, source_target_pairs={{0,12},{1,13},{2,14},{3,15},{4,0},{5,1},{6,2},{7,3},{8,4},{9,5},{1... | collective-permute-start | bytes 786440 | tf_op jit(solution)/shard_map/ppermute | solution.py:29
  62.1 27.8 %collective-permute-start.9 = (bf16[2,4,2,32,512]{4,3,2,1,0:T(8,128)(2,1)S(1)}, bf16[2,4,2,32,512]{4,3,2,1,0:T(8,128)(2,1)S(1)}, u32[]{:S(2)}, u32[]{:S(2)}) collective-permute-start(bf16[2,4,2,32,512]{4,3,2,1,0:T(8,128)(2,1)S(1)} %slice.141), channel_id=1, source_target_pairs={{0,96},{16,112},{32,0},{48,16},{64,32},{80,48},{96,64},{112,80},{1... | collective-permute-start | bytes 1572872 | tf_op jit(solution)/shard_map/ppermute | solution.py:15
  63.7 48.8 %collective-permute-start.16 = (bf16[4,4,2,32,512]{4,3,2,1,0:T(8,128)(2,1)S(1)}, bf16[4,4,2,32,512]{4,3,2,1,0:T(8,128)(2,1)S(1)}, u32[]{:S(2)}, u32[]{:S(2)}) collective-permute-start(bf16[4,4,2,32,512]{4,3,2,1,0:T(8,128)(2,1)S(1)} %get-tuple-element.22), channel_id=1, source_target_pairs={{0,16},{16,0},{32,48},{48,32},{64,80},{80,64},{96,112},{112,96},{1... | collective-permute-start | bytes 3145736 | tf_op jit(solution)/shard_map/ppermute | solution.py:19
  87.3 24.5 %collective-permute-start.34 = (bf16[4,4,2,32,512]{4,3,2,1,0:T(8,128)(2,1)S(1)}, bf16[4,4,2,32,512]{4,3,2,1,0:T(8,128)(2,1)S(1)}, u32[]{:S(2)}, u32[]{:S(2)}) collective-permute-start(bf16[4,4,2,32,512]{4,3,2,1,0:T(8,128)(2,1)S(1)} %pad_maximum_fusion.3), channel_id=1, source_target_pairs={{0,4},{1,5},{2,6},{3,7},{4,8},{5,9},{6,10},{7,11},{8,12},{9,13},{1... | collective-permute-start | bytes 3145736 | tf_op jit(solution)/shard_map/ppermute | solution.py:29
  88.0 27.3 %collective-permute-start.17 = (bf16[4,4,2,32,512]{4,3,2,1,0:T(8,128)(2,1)S(1)}, bf16[4,4,2,32,512]{4,3,2,1,0:T(8,128)(2,1)S(1)}, u32[]{:S(2)}, u32[]{:S(2)}) collective-permute-start(bf16[4,4,2,32,512]{4,3,2,1,0:T(8,128)(2,1)S(1)} %collective-permute-done.6), channel_id=1, source_target_pairs={{0,16},{16,0},{32,48},{48,32},{64,80},{80,64},{96,112},{112,96},{1... | collective-permute-start | bytes 3145736 | tf_op jit(solution)/shard_map/ppermute | solution.py:19
  89.9 25.4 %collective-permute-start.18 = (bf16[4,4,2,32,512]{4,3,2,1,0:T(8,128)(2,1)S(1)}, bf16[4,4,2,32,512]{4,3,2,1,0:T(8,128)(2,1)S(1)}, u32[]{:S(2)}, u32[]{:S(2)}) collective-permute-start(bf16[4,4,2,32,512]{4,3,2,1,0:T(8,128)(2,1)S(1)} %collective-permute-done.7), channel_id=1, source_target_pairs={{0,16},{16,0},{32,48},{48,32},{64,80},{80,64},{96,112},{112,96},{1... | collective-permute-start | bytes 3145736 | tf_op jit(solution)/shard_map/ppermute | solution.py:19
  90.0 27.9 %collective-permute-start.19 = (bf16[4,4,2,32,512]{4,3,2,1,0:T(8,128)(2,1)S(1)}, bf16[4,4,2,32,512]{4,3,2,1,0:T(8,128)(2,1)S(1)}, u32[]{:S(2)}, u32[]{:S(2)}) collective-permute-start(bf16[4,4,2,32,512]{4,3,2,1,0:T(8,128)(2,1)S(1)} %constant_dynamic-update-slice_fusion), channel_id=1, source_target_pairs={{0,16},{16,0},{32,48},{48,32},{64,80},{80,64},{96,112},{112,96},{1... | collective-permute-start | bytes 3145736 | tf_op jit(solution)/shard_map/ppermute | solution.py:19
  111.8 23.6 %collective-permute-start.24 = (bf16[4,4,2,32,512]{4,3,2,1,0:T(8,128)(2,1)S(1)}, bf16[4,4,2,32,512]{4,3,2,1,0:T(8,128)(2,1)S(1)}, u32[]{:S(2)}, u32[]{:S(2)}) collective-permute-start(bf16[4,4,2,32,512]{4,3,2,1,0:T(8,128)(2,1)S(1)} %pad_maximum_fusion.1), channel_id=1, source_target_pairs={{0,4},{1,5},{2,6},{3,7},{4,8},{5,9},{6,10},{7,11},{8,12},{9,13},{1... | collective-permute-start | bytes 3145736 | tf_op jit(solution)/shard_map/ppermute | solution.py:29
  112.5 22.9 %collective-permute-start.32 = (bf16[4,4,2,32,512]{4,3,2,1,0:T(8,128)(2,1)S(1)}, bf16[4,4,2,32,512]{4,3,2,1,0:T(8,128)(2,1)S(1)}, u32[]{:S(2)}, u32[]{:S(2)}) collective-permute-start(bf16[4,4,2,32,512]{4,3,2,1,0:T(8,128)(2,1)S(1)} %pad_maximum_fusion.3), channel_id=1, source_target_pairs={{0,12},{1,13},{2,14},{3,15},{4,0},{5,1},{6,2},{7,3},{8,4},{9,5},{1... | collective-permute-start | bytes 3145736 | tf_op jit(solution)/shard_map/ppermute | solution.py:29
  115.3 23.1 %collective-permute-start.25 = (bf16[4,4,2,32,512]{4,3,2,1,0:T(8,128)(2,1)S(1)}, bf16[4,4,2,32,512]{4,3,2,1,0:T(8,128)(2,1)S(1)}, u32[]{:S(2)}, u32[]{:S(2)}) collective-permute-start(bf16[4,4,2,32,512]{4,3,2,1,0:T(8,128)(2,1)S(1)} %pad_maximum_fusion.2), channel_id=1, source_target_pairs={{0,1},{1,2},{2,3},{3,0},{4,5},{5,6},{6,7},{7,4},{8,9},{9,10},{10,1... | collective-permute-start | bytes 3145736 | tf_op jit(solution)/shard_map/ppermute | solution.py:24
  115.3 24.9 %collective-permute-start.27 = (bf16[4,4,2,32,512]{4,3,2,1,0:T(8,128)(2,1)S(1)}, bf16[4,4,2,32,512]{4,3,2,1,0:T(8,128)(2,1)S(1)}, u32[]{:S(2)}, u32[]{:S(2)}) collective-permute-start(bf16[4,4,2,32,512]{4,3,2,1,0:T(8,128)(2,1)S(1)} %pad_maximum_fusion.2), channel_id=1, source_target_pairs={{0,3},{1,0},{2,1},{3,2},{4,7},{5,4},{6,5},{7,6},{8,11},{9,8},{10,9... | collective-permute-start | bytes 3145736 | tf_op jit(solution)/shard_map/ppermute | solution.py:24
  118.0 41.8 %collective-permute-start.33 = (bf16[4,4,2,32,512]{4,3,2,1,0:T(8,128)(2,1)S(1)}, bf16[4,4,2,32,512]{4,3,2,1,0:T(8,128)(2,1)S(1)}, u32[]{:S(2)}, u32[]{:S(2)}) collective-permute-start(bf16[4,4,2,32,512]{4,3,2,1,0:T(8,128)(2,1)S(1)} %pad_maximum_fusion.4), channel_id=1, source_target_pairs={{0,3},{1,0},{2,1},{3,2},{4,7},{5,4},{6,5},{7,6},{8,11},{9,8},{10,9... | collective-permute-start | bytes 3145736 | tf_op jit(solution)/shard_map/ppermute | solution.py:24
  135.4 30.9 %collective-permute-start.35 = (bf16[4,4,2,32,512]{4,3,2,1,0:T(8,128)(2,1)S(1)}, bf16[4,4,2,32,512]{4,3,2,1,0:T(8,128)(2,1)S(1)}, u32[]{:S(2)}, u32[]{:S(2)}) collective-permute-start(bf16[4,4,2,32,512]{4,3,2,1,0:T(8,128)(2,1)S(1)} %pad_maximum_fusion.4), channel_id=1, source_target_pairs={{0,1},{1,2},{2,3},{3,0},{4,5},{5,6},{6,7},{7,4},{8,9},{9,10},{10,1... | collective-permute-start | bytes 3145736 | tf_op jit(solution)/shard_map/ppermute | solution.py:24
  135.4 50.3 %collective-permute-start.28 = (bf16[4,4,2,32,512]{4,3,2,1,0:T(8,128)(2,1)S(1)}, bf16[4,4,2,32,512]{4,3,2,1,0:T(8,128)(2,1)S(1)}, u32[]{:S(2)}, u32[]{:S(2)}) collective-permute-start(bf16[4,4,2,32,512]{4,3,2,1,0:T(8,128)(2,1)S(1)} %collective-permute-done.24), channel_id=1, source_target_pairs={{0,4},{1,5},{2,6},{3,7},{4,8},{5,9},{6,10},{7,11},{8,12},{9,13},{1... | collective-permute-start | bytes 3145736 | tf_op jit(solution)/shard_map/ppermute | solution.py:29
  138.3 48.2 %collective-permute-start.36 = (bf16[4,4,2,32,512]{4,3,2,1,0:T(8,128)(2,1)S(1)}, bf16[4,4,2,32,512]{4,3,2,1,0:T(8,128)(2,1)S(1)}, u32[]{:S(2)}, u32[]{:S(2)}) collective-permute-start(bf16[4,4,2,32,512]{4,3,2,1,0:T(8,128)(2,1)S(1)} %collective-permute-done.32), channel_id=1, source_target_pairs={{0,12},{1,13},{2,14},{3,15},{4,0},{5,1},{6,2},{7,3},{8,4},{9,5},{1... | collective-permute-start | bytes 3145736 | tf_op jit(solution)/shard_map/ppermute | solution.py:29
  140.2 44.1 %collective-permute-start.29 = (bf16[4,4,2,32,512]{4,3,2,1,0:T(8,128)(2,1)S(1)}, bf16[4,4,2,32,512]{4,3,2,1,0:T(8,128)(2,1)S(1)}, u32[]{:S(2)}, u32[]{:S(2)}) collective-permute-start(bf16[4,4,2,32,512]{4,3,2,1,0:T(8,128)(2,1)S(1)} %collective-permute-done.25), channel_id=1, source_target_pairs={{0,1},{1,2},{2,3},{3,0},{4,5},{5,6},{6,7},{7,4},{8,9},{9,10},{10,1... | collective-permute-start | bytes 3145736 | tf_op jit(solution)/shard_map/ppermute | solution.py:24
  159.8 25.2 %collective-permute-start.37 = (bf16[4,4,2,32,512]{4,3,2,1,0:T(8,128)(2,1)S(1)}, bf16[4,4,2,32,512]{4,3,2,1,0:T(8,128)(2,1)S(1)}, u32[]{:S(2)}, u32[]{:S(2)}) collective-permute-start(bf16[4,4,2,32,512]{4,3,2,1,0:T(8,128)(2,1)S(1)} %collective-permute-done.33), channel_id=1, source_target_pairs={{0,3},{1,0},{2,1},{3,2},{4,7},{5,4},{6,5},{7,6},{8,11},{9,8},{10,9... | collective-permute-start | bytes 3145736 | tf_op jit(solution)/shard_map/ppermute | solution.py:24
  (14 other events, 149.8 us)
